TPU v7x, 32 devices: a whole 2x2x4 slice. The times are simulated.
32 devices in a mesh: groups: 2 (over y), tile: 4 (over z), col: 2 (over x), rep: 2 (over core).
Axes of the slice: x: 2, y: 2, z: 4, core: 2. Of those that a mesh axis runs over, the one named last changes fastest.
Arguments:
- forcing: bfloat16 [4, 20, 32, 2048], P(('groups', 'rep'), 'tile', None, 'col'), parts along dimension 0, may hold values from -6 to 6
- member_kernel_weight: bfloat16 [20, 576, 64], P('tile'), may hold values from -0.25 to 0.25
- member_counts: int32 [4], P('tile'), may hold values from 1 to 5, 16 in all
- mixing_input_weight: bfloat16 [1280, 512], P('tile'), may hold values from -0.1875 to 0.1875
- depth_weight: float32 [9, 512], replicated, may hold values from -2 to 2
- mix_weight: bfloat16 [512, 512], replicated, may hold values from -0.25 to 0.25
- cotangent: bfloat16 [4, 32, 32, 512], P(('groups', 'rep'), 'tile', 'col'), parts along dimension 0, may hold values from -6 to 6
Outputs:
- adjusted: bfloat16 [4, 32, 32, 512], P(('groups', 'rep'), 'tile', 'col'), parts along dimension 0
- mix_grad: float32 [1024, 512], P(('groups', 'tile', 'col', 'rep')), parts along dimension 0
- depth_grad: float32 [18, 512], P('groups'), parts along dimension 0
- in_grad: float32 [2560, 512], P(('groups', 'tile')), parts along dimension 0
- group_grad: float32 [40, 576, 64], P(('groups', 'tile')), parts along dimension 0
There are 2 independent parts, one for each index of `groups`. A program takes and returns all parts, laid end to end along the dimension named above; an argument that names none is the same for every part. Nothing has to cross between parts.
Inputs may be any that keep to these rules, and one draw needn't show every extreme that they name: member_counts sums to 16; each index of tile holds at least one member and at least one holds 5.
All inputs are finite; a program needn't handle non-finite values. No bound on the sum of `member_counts` on one device may be relied on, other than what follows from the above.
Results may differ from a plain program's by a relative error of at most 0.011.
Values may be sent and summed in bfloat16 or wider, within the bound.
No kernel may reach another device: no remote copies, remote signals or barrier semaphores. Data moves between devices by JAX's collectives and lax.ppermute only.
A program may use at most 64 MiB of HBM per device.

v0:
```python
import jax
import jax.numpy as jnp
from jax import lax
from jax.sharding import PartitionSpec as P


def extended_2(block, sides, width):
    for axis, dim in sides:
        count = lax.axis_size(axis)
        forward = [(i, i + 1) for i in range(count - 1)]
        backward = [(target, source) for source, target in forward]
        low = lax.ppermute(
            lax.slice_in_dim(block, block.shape[dim] - width, None, axis=dim), axis, forward
        )
        high = lax.ppermute(lax.slice_in_dim(block, 0, width, axis=dim), axis, backward)
        block = jnp.concatenate([low, block, high], axis=dim)
    return block


def silu_slope(value):
    sig = jax.nn.sigmoid(value)
    return sig * (1.0 + value * (1.0 - sig))


def slot_patches(extended, slot, channels):
    height = extended.shape[1]
    width = extended.shape[2] // channels - 2
    field = lax.dynamic_index_in_dim(extended, slot, 0, keepdims=False).reshape(
        height, width + 2, channels
    )
    padded = jnp.pad(field, ((1, 1), (0, 0), (0, 0)))
    stacked = jnp.concatenate(
        [
            padded[down : down + height, across : across + width]
            for down in range(3)
            for across in range(3)
        ],
        axis=-1,
    )
    return stacked.reshape(height * width, 9 * channels)


def fetch_weight(mixing_input_weight):
    full_weight = lax.all_gather(mixing_input_weight, "tile", axis=0, tiled=True)
    return full_weight


def local(
    forcing,
    member_kernel_weight,
    member_counts,
    mixing_input_weight,
    depth_weight,
    mix_weight,
    cotangent,
):
    channels = member_kernel_weight.shape[2]
    slots_here = forcing.shape[1]
    height = forcing.shape[2]
    width = forcing.shape[3] // channels
    hidden_width = mixing_input_weight.shape[1]
    slot_width = slots_here * channels
    count = member_counts[0]
    band = height // lax.axis_size("tile")
    extended = extended_2(forcing, (("col", 3),), channels)[0]

    def forward_slot(slot, buffer):
        columns = slot_patches(extended, slot, channels)
        weight = lax.dynamic_index_in_dim(member_kernel_weight, slot, 0, keepdims=False)
        gate = jnp.dot(columns, weight, preferred_element_type=jnp.float32)
        result = jax.nn.silu(gate).astype(jnp.bfloat16).reshape(height, width, channels)
        return lax.dynamic_update_slice_in_dim(buffer, result, slot * channels, 2)

    feature_maps = lax.fori_loop(
        0, count, forward_slot, jnp.zeros((height, width, slot_width), jnp.bfloat16)
    )
    full_weight = None
    gathered = lax.all_to_all(feature_maps, "tile", split_axis=0, concat_axis=2, tiled=True)
    all_width = gathered.shape[2]
    full_weight = fetch_weight(mixing_input_weight)
    mixed_in = jnp.dot(
        gathered.reshape(-1, all_width), full_weight, preferred_element_type=jnp.float32
    )
    mixed_in = mixed_in.astype(jnp.bfloat16).reshape(band, width, hidden_width)
    act_pad = extended_2(mixed_in, (("tile", 0), ("col", 1)), 1)
    before = jnp.zeros((band, width, hidden_width), jnp.float32)
    for down in range(3):
        for across in range(3):
            before = before + depth_weight[down * 3 + across] * act_pad[
                down : down + band, across : across + width
            ].astype(jnp.float32)
    hidden = jax.nn.silu(before).astype(jnp.bfloat16)
    flat_hidden = hidden.reshape(-1, hidden_width)
    adjusted = jnp.dot(flat_hidden, mix_weight.T, preferred_element_type=jnp.float32).astype(
        jnp.bfloat16
    )
    adjusted = adjusted.reshape(1, band, width, hidden_width)
    upstream = cotangent[0].reshape(-1, hidden_width)
    hidden_grad = jnp.dot(upstream, mix_weight, preferred_element_type=jnp.float32).reshape(
        band, width, hidden_width
    )
    before_grad = (hidden_grad * silu_slope(before)).astype(jnp.bfloat16)
    mix_grad = lax.psum_scatter(
        jnp.dot(upstream.T, flat_hidden, preferred_element_type=jnp.float32),
        ("tile", "col", "rep"),
        scatter_dimension=0,
        tiled=True,
    )
    grad_wide = before_grad.astype(jnp.float32)
    depth_terms = jnp.stack(
        [
            jnp.sum(
                act_pad[down : down + band, across : across + width].astype(jnp.float32)
                * grad_wide,
                axis=(0, 1),
            )
            for down in range(3)
            for across in range(3)
        ],
        axis=0,
    )
    depth_grad = lax.psum(depth_terms, ("tile", "col", "rep"))
    grad_pad = extended_2(before_grad, (("tile", 0), ("col", 1)), 1)
    act_grad = jnp.zeros((band, width, hidden_width), jnp.float32)
    for down in range(3):
        for across in range(3):
            act_grad = act_grad + depth_weight[down * 3 + across] * grad_pad[
                2 - down : 2 - down + band, 2 - across : 2 - across + width
            ].astype(jnp.float32)
    act_grad = act_grad.astype(jnp.bfloat16)
    piece = lax.all_gather(act_grad, "tile", axis=0, tiled=True)
    number = piece.shape[0]
    flat_piece = piece.reshape(-1, hidden_width)
    rows_here = feature_maps.reshape(-1, slot_width)
    weight_total = jnp.dot(rows_here.T, flat_piece, preferred_element_type=jnp.float32)
    block = jnp.dot(flat_piece, mixing_input_weight.T, preferred_element_type=jnp.float32).astype(
        jnp.bfloat16
    )
    buffer = block.reshape(number, width, slot_width)
    feature_gradient = buffer
    in_grad = lax.psum(weight_total.astype(jnp.bfloat16), ("col", "rep")).astype(jnp.float32)

    def backward_slot(slot, totals):
        columns = slot_patches(extended, slot, channels)
        weight = lax.dynamic_index_in_dim(member_kernel_weight, slot, 0, keepdims=False)
        gate = jnp.dot(columns, weight, preferred_element_type=jnp.float32)
        slot_grad = lax.dynamic_slice_in_dim(
            feature_gradient, slot * channels, channels, 2
        ).reshape(-1, channels)
        inner = (slot_grad.astype(jnp.float32) * silu_slope(gate)).astype(jnp.bfloat16)
        term = jnp.dot(columns.T, inner, preferred_element_type=jnp.float32)
        return lax.dynamic_update_index_in_dim(totals, term, slot, 0)

    group_term = lax.fori_loop(
        0, count, backward_slot, jnp.zeros((slots_here, 9 * channels, channels), jnp.float32)
    )
    group_grad = lax.psum(group_term.astype(jnp.bfloat16), ("col", "rep")).astype(jnp.float32)
    return (adjusted, mix_grad, depth_grad, in_grad, group_grad)


def solution(mesh):
    in_specs = (
        P(("groups", "rep"), "tile", None, "col"),
        P("tile", None, None),
        P("tile"),
        P("tile", None),
        P(),
        P(),
        P(("groups", "rep"), "tile", "col", None),
    )
    out_specs = (
        P(("groups", "rep"), "tile", "col", None),
        P(("groups", "tile", "col", "rep"), None),
        P("groups", None),
        P(("groups", "tile"), None),
        P(("groups", "tile"), None, None),
    )
    return jax.shard_map(local, mesh=mesh, in_specs=in_specs, out_specs=out_specs, check_vma=False)
```

profile of v0, /device:TPU:0, one launch (start us, length us, event | category | flops | bytes accessed | tf_op | source)
XLA Modules:
  0.0 233.5 jit_solution(2599027453419804770)
XLA Ops:
  8.2 4.9 %collective-permute-start = (bf16[1,5,32,64]{3,2,1,0:T(8,128)(2,1)S(1)}, bf16[1,5,32,64]{3,2,1,0:T(8,128)(2,1)S(1)}, u32[]{:S(2)}, u32[]{:S(2)}) collective-permute-start(bf16[1,5,32,64]{3,2,1,0:T(8,128)(2,1)S(1)} %get-tuple-element.229), channel_id=1, source_target_pairs={{0,2},{1,3},{4,6},{5,7},{8,10},{9,11},{12,14},{13,15},{16,18},{17,... | collective-permute-start | bytes 61448 | tf_op jit(solution)/shard_map/ppermute | solution.py:12
  13.0 1.3 collective-permute-start.1
  14.7 4.2 %collective-permute-done.1 = bf16[1,5,32,64]{3,2,1,0:T(8,128)(2,1)S(1)} collective-permute-done((bf16[1,5,32,64]{3,2,1,0:T(8,128)(2,1)S(1)}, bf16[1,5,32,64]{3,2,1,0:T(8,128)(2,1)S(1)}, u32[]{:S(2)}, u32[]{:S(2)}) %collective-permute-start.1) | collective-permute-done | bytes 20512 | tf_op jit(solution)/shard_map/ppermute | solution.py:15
  18.9 1.3 concatenate.55
  20.3 27.4 %while.24 = (s32[]{:T(128)}, bf16[32,16,320]{2,1,0:T(8,128)(2,1)S(1)}, s32[]{:T(128)}, bf16[5,32,1152]{2,1,0:T(8,128)(2,1)S(1)}, bf16[5,576,64]{1,2,0:T(8,128)(2...) while((s32[]{:T(128)}, bf16[32,16,320]{2,1,0:T(8,128)(2,1)S(1)}, s32[]{:T(128)}, ...), condition=%wide.region_1.2_spmd, body=%wide.region_0.1_spmd.sunk | while | flops 37912580 | bytes 3653833 | solution.py:74
  26.8 5.0 %dynamic_update_slice.16 = bf16[32,16,320]{2,1,0:T(8,128)(2,1)S(1)} dynamic-update-slice(bf16[32,16,320]{2,1,0:T(8,128)(2,1)S(1)} %get-tuple-element.369, bf16[32,16,64]{2,1,0:T(8,128)(2,1)S(1)} %bitcast.109, s32[]{:T(128)} %constant.90.clone.1..sunk, s32[]{:T(128)} %constant.90.clone.1..sunk, s32[]{:T(128)S(6)} %select_n.35) | dynamic-update-slice | bytes 131076 | tf_op jit(solution)/shard_map/while/body/dynamic_update_slice | solution.py:72
  38.5 5.0 %dynamic_update_slice.16 = bf16[32,16,320]{2,1,0:T(8,128)(2,1)S(1)} dynamic-update-slice(bf16[32,16,320]{2,1,0:T(8,128)(2,1)S(1)} %get-tuple-element.369, bf16[32,16,64]{2,1,0:T(8,128)(2,1)S(1)} %bitcast.109, s32[]{:T(128)} %constant.90.clone.1..sunk, s32[]{:T(128)} %constant.90.clone.1..sunk, s32[]{:T(128)S(6)} %select_n.35) | dynamic-update-slice | bytes 131076 | tf_op jit(solution)/shard_map/while/body/dynamic_update_slice | solution.py:72
  47.7 12.9 %all_to_all.15 = bf16[32,16,320]{2,1,0:T(8,128)(2,1)S(1)} all-to-all(bf16[32,16,320]{2,1,0:T(8,128)(2,1)S(1)} %get-tuple-element.153), channel_id=1, replica_groups=mesh['groups'=2,'tile'=4,'col'=2,'rep'=2] {'tile'}, dimensions={0} | all-to-all | bytes 655360 | tf_op jit(solution)/shard_map/all_to_all | solution.py:78
  61.3 1.7 convolution_convert_fusion.2
  63.0 1.4 collective-permute-start.3
  64.4 4.5 %collective-permute-start.2 = (bf16[1,16,512]{2,1,0:T(8,128)(2,1)S(1)}, bf16[1,16,512]{2,1,0:T(8,128)(2,1)S(1)}, u32[]{:S(2)}, u32[]{:S(2)}) collective-permute-start(bf16[1,16,512]{2,1,0:T(8,128)(2,1)S(1)} %get-tuple-element.240), channel_id=1, source_target_pairs={{0,4},{4,8},{8,12},{1,5},{5,9},{9,13},{2,6},{6,10},{10,14},{3,7},{... | collective-permute-start | bytes 49160 | tf_op jit(solution)/shard_map/ppermute | solution.py:12
  69.0 1.4 collective-permute-done.2
  70.4 1.9 collective-permute-start.4
  72.4 1.3 collective-permute-start.5
  73.8 4.2 %collective-permute-done.5 = bf16[10,1,512]{2,1,0:T(2,128)(2,1)S(1)} collective-permute-done((bf16[10,1,512]{2,1,0:T(2,128)(2,1)S(1)}, bf16[10,1,512]{2,1,0:T(2,128)(2,1)S(1)}, u32[]{:S(2)}, u32[]{:S(2)}) %collective-permute-start.5) | collective-permute-done | bytes 10272 | tf_op jit(solution)/shard_map/ppermute | solution.py:15
  81.5 4.8 %collective-permute-start.6 = (bf16[1,16,512]{2,1,0:T(8,128)(2,1)S(1)}, bf16[1,16,512]{2,1,0:T(8,128)(2,1)S(1)}, u32[]{:S(2)}, u32[]{:S(2)}) collective-permute-start(bf16[1,16,512]{2,1,0:T(8,128)(2,1)S(1)} %get-tuple-element.238), channel_id=1, source_target_pairs={{0,4},{4,8},{8,12},{1,5},{5,9},{9,13},{2,6},{6,10},{10,14},{3,7},{... | collective-permute-start | bytes 49160 | tf_op jit(solution)/shard_map/ppermute | solution.py:12
  86.4 1.4 collective-permute-done.6
  87.8 1.3 collective-permute-start.8
  89.1 4.5 %collective-permute-start.9 = (bf16[10,1,512]{2,1,0:T(2,128)(2,1)S(1)}, bf16[10,1,512]{2,1,0:T(2,128)(2,1)S(1)}, u32[]{:S(2)}, u32[]{:S(2)}) collective-permute-start(bf16[10,1,512]{2,1,0:T(2,128)(2,1)S(1)} %get-tuple-element.233), channel_id=1, source_target_pairs={{0,2},{1,3},{4,6},{5,7},{8,10},{9,11},{12,14},{13,15},{16,18},{17,... | collective-permute-start | bytes 30728 | tf_op jit(solution)/shard_map/ppermute | solution.py:12
  93.7 1.5 collective-permute-done.9
  95.5 16.0 %all_gather.7 = bf16[32,16,512]{2,1,0:T(8,128)(2,1)S(1)} all-gather(bf16[8,16,512]{2,1,0:T(8,128)(2,1)S(1)} %fusion.44), channel_id=1, replica_groups=mesh['groups'=2,'tile'=4,'col'=2,'rep'=2] {'tile'}, dimensions={0}, use_global_device_ids=true | all-gather | bytes 655360 | tf_op jit(solution)/shard_map/all_gather | solution.py:131
  113.2 16.9 %while.25 = (s32[]{:T(128)}, bf16[5,576,64]{1,2,0:T(8,128)(2,1)S(1)}, s32[]{:T(128)}, bf16[5,32,1152]{2,1,0:T(8,128)(2,1)S(1)}, bf16[32,16,320]{2,1,0:T(8,128)(2...) while((s32[]{:T(128)}, ...), condition=%wide.region_15.16_spmd, body=%wide.region_14.15_spmd.sunk | while | flops 75825160 | bytes 4932813 | solution.py:154
  115.1 1.4 fusion.74
  118.3 1.4 fusion.74
  121.6 1.4 fusion.74
  124.8 1.4 fusion.74
  128.1 1.4 fusion.74
  132.3 1.3 copy.27
  133.8 58.4 %psum.21 = f32[9,512]{1,0:T(8,128)} all-reduce(f32[9,512]{1,0:T(8,128)S(1)} %stack.39), channel_id=1, replica_groups=mesh['groups'=2,'tile'=4,'col'=2,'rep'=2] {'tile','col','rep'}, use_global_device_ids=true, to_apply=%region_12.13 | all-reduce | flops 4608 | bytes 36864 | tf_op jit(solution)/shard_map/psum | solution.py:122
  193.1 1.9 convert_element_type.146
  195.0 1.9 convert_element_type.149
  196.9 30.0 %reduce-scatter.4.cloned.1.call-done = f32[32,512]{1,0:T(8,128)} async-done(((f32[512,512]{1,0:T(8,128)}), f32[32,512]{1,0:T(8,128)}) %reduce-scatter.4.cloned.1.call-update) | async-done | bytes 65552
  (121 shorter events, 29.5 us)
Async XLA Ops:
  7.2 71.9 %copy-start = (bf16[512,512]{1,0:T(8,128)(2,1)S(1)}, bf16[512,512]{1,0:T(8,128)(2,1)}, u32[]{:S(2)}) copy-start(bf16[512,512]{1,0:T(8,128)(2,1)} %param.16) | copy-start | bytes 1572868
  7.2 54.1 %all-gather.2.cloned.1.call-start = ((), (), s32[]{:S(2)}) async-start(), calls=%async_computation.2 | async-start | bytes 1638400 | tf_op jit(solution)/shard_map/all_gather | solution.py:44
  8.2 6.5 %collective-permute-start = (bf16[1,5,32,64]{3,2,1,0:T(8,128)(2,1)S(1)}, bf16[1,5,32,64]{3,2,1,0:T(8,128)(2,1)S(1)}, u32[]{:S(2)}, u32[]{:S(2)}) collective-permute-start(bf16[1,5,32,64]{3,2,1,0:T(8,128)(2,1)S(1)} %get-tuple-element.229), channel_id=1, source_target_pairs={{0,2},{1,3},{4,6},{5,7},{8,10},{9,11},{12,14},{13,15},{16,18},{17,... | collective-permute-start | bytes 61448 | tf_op jit(solution)/shard_map/ppermute | solution.py:12
  13.0 5.9 %collective-permute-start.1 = (bf16[1,5,32,64]{3,2,1,0:T(8,128)(2,1)S(1)}, bf16[1,5,32,64]{3,2,1,0:T(8,128)(2,1)S(1)}, u32[]{:S(2)}, u32[]{:S(2)}) collective-permute-start(bf16[1,5,32,64]{3,2,1,0:T(8,128)(2,1)S(1)} %get-tuple-element.228), channel_id=1, source_target_pairs={{2,0},{3,1},{6,4},{7,5},{10,8},{11,9},{14,12},{15,13},{18,16},{19,... | collective-permute-start | bytes 61448 | tf_op jit(solution)/shard_map/ppermute | solution.py:15
  14.4 178.7 %all-reduce.5.cloned.1.call-start = ((), (), s32[]{:S(2)}) async-start(), calls=%async_computation.4 | async-start | bytes 1474560 | tf_op jit(solution)/shard_map/psum | solution.py:141
  60.9 12.7 %copy-start.5 = (f32[9,512]{1,0:T(8,128)S(1)}, f32[9,512]{1,0:T(8,128)}, u32[]{:S(2)}) copy-start(f32[9,512]{1,0:T(8,128)} %param.15) | copy-start | bytes 55300
  63.0 16.1 %copy-start.4 = (bf16[1,8,16,512]{3,2,1,0:T(8,128)(2,1)S(1)}, bf16[1,8,16,512]{3,2,1,0:T(8,128)(2,1)}, u32[]{:S(2)}) copy-start(bf16[1,8,16,512]{3,2,1,0:T(8,128)(2,1)} %param.17) | copy-start | bytes 393220
  63.0 6.0 %collective-permute-start.3 = (bf16[1,16,512]{2,1,0:T(8,128)(2,1)S(1)}, bf16[1,16,512]{2,1,0:T(8,128)(2,1)S(1)}, u32[]{:S(2)}, u32[]{:S(2)}) collective-permute-start(bf16[1,16,512]{2,1,0:T(8,128)(2,1)S(1)} %get-tuple-element.241), channel_id=1, source_target_pairs={{4,0},{8,4},{12,8},{5,1},{9,5},{13,9},{6,2},{10,6},{14,10},{7,3},{... | collective-permute-start | bytes 49160 | tf_op jit(solution)/shard_map/ppermute | solution.py:15
  64.4 6.0 %collective-permute-start.2 = (bf16[1,16,512]{2,1,0:T(8,128)(2,1)S(1)}, bf16[1,16,512]{2,1,0:T(8,128)(2,1)S(1)}, u32[]{:S(2)}, u32[]{:S(2)}) collective-permute-start(bf16[1,16,512]{2,1,0:T(8,128)(2,1)S(1)} %get-tuple-element.240), channel_id=1, source_target_pairs={{0,4},{4,8},{8,12},{1,5},{5,9},{9,13},{2,6},{6,10},{10,14},{3,7},{... | collective-permute-start | bytes 49160 | tf_op jit(solution)/shard_map/ppermute | solution.py:12
  70.4 3.4 %collective-permute-start.4 = (bf16[10,1,512]{2,1,0:T(2,128)(2,1)S(1)}, bf16[10,1,512]{2,1,0:T(2,128)(2,1)S(1)}, u32[]{:S(2)}, u32[]{:S(2)}) collective-permute-start(bf16[10,1,512]{2,1,0:T(2,128)(2,1)S(1)} %get-tuple-element.236), channel_id=1, source_target_pairs={{0,2},{1,3},{4,6},{5,7},{8,10},{9,11},{12,14},{13,15},{16,18},{17,... | collective-permute-start | bytes 30728 | tf_op jit(solution)/shard_map/ppermute | solution.py:12
  72.4 5.7 %collective-permute-start.5 = (bf16[10,1,512]{2,1,0:T(2,128)(2,1)S(1)}, bf16[10,1,512]{2,1,0:T(2,128)(2,1)S(1)}, u32[]{:S(2)}, u32[]{:S(2)}) collective-permute-start(bf16[10,1,512]{2,1,0:T(2,128)(2,1)S(1)} %get-tuple-element.237), channel_id=1, source_target_pairs={{2,0},{3,1},{6,4},{7,5},{10,8},{11,9},{14,12},{15,13},{18,16},{19,... | collective-permute-start | bytes 30728 | tf_op jit(solution)/shard_map/ppermute | solution.py:15
  80.2 6.1 %collective-permute-start.7 = (bf16[1,16,512]{2,1,0:T(8,128)(2,1)S(1)}, bf16[1,16,512]{2,1,0:T(8,128)(2,1)S(1)}, u32[]{:S(2)}, u32[]{:S(2)}) collective-permute-start(bf16[1,16,512]{2,1,0:T(8,128)(2,1)S(1)} %get-tuple-element.239), channel_id=1, source_target_pairs={{4,0},{8,4},{12,8},{5,1},{9,5},{13,9},{6,2},{10,6},{14,10},{7,3},{... | collective-permute-start | bytes 49160 | tf_op jit(solution)/shard_map/ppermute | solution.py:15
  81.5 6.3 %collective-permute-start.6 = (bf16[1,16,512]{2,1,0:T(8,128)(2,1)S(1)}, bf16[1,16,512]{2,1,0:T(8,128)(2,1)S(1)}, u32[]{:S(2)}, u32[]{:S(2)}) collective-permute-start(bf16[1,16,512]{2,1,0:T(8,128)(2,1)S(1)} %get-tuple-element.238), channel_id=1, source_target_pairs={{0,4},{4,8},{8,12},{1,5},{5,9},{9,13},{2,6},{6,10},{10,14},{3,7},{... | collective-permute-start | bytes 49160 | tf_op jit(solution)/shard_map/ppermute | solution.py:12
  87.8 5.9 %collective-permute-start.8 = (bf16[10,1,512]{2,1,0:T(2,128)(2,1)S(1)}, bf16[10,1,512]{2,1,0:T(2,128)(2,1)S(1)}, u32[]{:S(2)}, u32[]{:S(2)}) collective-permute-start(bf16[10,1,512]{2,1,0:T(2,128)(2,1)S(1)} %get-tuple-element.232), channel_id=1, source_target_pairs={{2,0},{3,1},{6,4},{7,5},{10,8},{11,9},{14,12},{15,13},{18,16},{19,... | collective-permute-start | bytes 30728 | tf_op jit(solution)/shard_map/ppermute | solution.py:15
  89.1 6.0 %collective-permute-start.9 = (bf16[10,1,512]{2,1,0:T(2,128)(2,1)S(1)}, bf16[10,1,512]{2,1,0:T(2,128)(2,1)S(1)}, u32[]{:S(2)}, u32[]{:S(2)}) collective-permute-start(bf16[10,1,512]{2,1,0:T(2,128)(2,1)S(1)} %get-tuple-element.233), channel_id=1, source_target_pairs={{0,2},{1,3},{4,6},{5,7},{8,10},{9,11},{12,14},{13,15},{16,18},{17,... | collective-permute-start | bytes 30728 | tf_op jit(solution)/shard_map/ppermute | solution.py:12
  111.5 1.1 copy-start.2
  130.2 0.8 copy-start.1
  131.0 96.0 %reduce-scatter.4.cloned.1.call-start = ((), (), s32[]{:S(2)}) async-start(), calls=%async_computation.3 | async-start | bytes 1114112
  132.3 1.4 copy-start.6
  132.3 1.4 copy-start.7
  132.3 1.4 copy-start.8
  132.3 59.8 %copy-start.3 = (bf16[8,16,512]{2,1,0:T(8,128)(2,1)S(1)}, bf16[8,16,512]{2,1,0:T(8,128)(2,1)}, u32[]{:S(2)}) copy-start(bf16[8,16,512]{2,1,0:T(8,128)(2,1)} %get-tuple-element.208) | copy-start | bytes 393220
Sparse Core Ops, SparseCore 0:
  14.5 34.9 all-gather.1
  131.1 33.7 all-reduce.4
  169.0 57.8 reduce-scatter.3
where the time goes:
time: 235 us; the launch traced here: 233 us
  blocking collectives  87.3 us (37%)
  waiting for transfers between devices  43.2 us (18%)
  local copies, waits for them, and re-layouts  27.7 us (12%)
  starting transfers between devices  27.4 us (12%)
  matrix products  19.9 us (8%)
  between operations  14.1 us (6%)
  loops' own time  8.51 us (4%)
  other arithmetic  5.39 us (2%)
    psum x1, blocking collectives, local(): depth_grad = lax.psum(depth_terms, ('tile', 'col', 'rep'))  58.4 us
    unnamed x4, waiting for transfers between devices  30.1 us
    ppermute x5, starting transfers between devices, extended_2(): lax.ppermute(lax.slice_in_dim(block, block.shape[dim] - width, None, axis...  20.7 us
    all_gather x1, blocking collectives, local(): piece = lax.all_gather(act_grad, 'tile', axis=0, tiled=True)  16 us
    all_to_all x1, blocking collectives, local(): lax.all_to_all(feature_maps, 'tile', split_axis=0, concat_axis=2, tiled=T...  12.9 us
    dynamic_update_slice x5, local copies, waits for them, and re-layouts, forward_slot(): return lax.dynamic_update_slice_in_dim(buffer, result, slot * channels, 2)  12.2 us
    ppermute x5, waiting for transfers between devices, extended_2(): lax.ppermute(lax.slice_in_dim(block, 0, width, axis=dim), axis, backward)  8.46 us
    dot_general x5, matrix products, backward_slot(): term = jnp.dot(columns.T, inner, preferred_element_type=jnp.float32)  7.15 us
  transfers between devices with their start and end apart: 13, of which 8 were waited for; matrix products, arithmetic and copies ran while one was open for 14% of the time, Pallas kernels for 0%

commit v1 on v0

--- a/solution.py
+++ b/solution.py
@@ -119,7 +119,7 @@
         ],
         axis=0,
     )
-    depth_grad = lax.psum(depth_terms, ("tile", "col", "rep"))
+    depth_grad = jnp.sum(lax.all_gather(depth_terms, ("tile", "col", "rep")), axis=0)
     grad_pad = extended_2(before_grad, (("tile", 0), ("col", 1)), 1)
     act_grad = jnp.zeros((band, width, hidden_width), jnp.float32)
     for down in range(3):

time: 235 us -> 236 us (level)
  waiting for transfers between devices: 43.2 us -> 81.9 us
  blocking collectives: 87.3 us -> 49.8 us
    psum x1 -> x0, blocking collectives: 58.4 us -> none  [local(): depth_grad = lax.psum(depth_terms, ('tile', 'col', 'rep'))]
    unnamed x4, waiting for transfers between devices: 30.1 us -> 58.3 us
    all_gather x0 -> x1, blocking collectives: none -> 20.8 us  [local(): lax.all_gather(depth_terms, ('tile', 'col', 'rep'))]
    psum x1, waiting for transfers between devices: 0.01 us -> 10.5 us  [local(): lax.psum(weight_total.astype(jnp.bfloat16), ('col', 'rep'))]
  transfers between devices with their start and end apart: 13 -> 13, of which waited for: 8 -> 9; matrix products, arithmetic and copies ran while one was open for 14% -> 14% of each run, Pallas kernels for 0% -> 0%
where the time goes in v1:
time: 236 us; the launch traced here: 235 us
  waiting for transfers between devices  81.9 us (35%)
  blocking collectives  49.8 us (21%)
  local copies, waits for them, and re-layouts  27.7 us (12%)
  starting transfers between devices  27.4 us (12%)
  matrix products  19.9 us (8%)
  between operations  14.1 us (6%)
  loops' own time  8.51 us (4%)
  other arithmetic  6.04 us (3%)
    unnamed x4, waiting for transfers between devices  58.3 us
    all_gather x1, blocking collectives, local(): lax.all_gather(depth_terms, ('tile', 'col', 'rep'))  20.8 us
    ppermute x5, starting transfers between devices, extended_2(): lax.ppermute(lax.slice_in_dim(block, block.shape[dim] - width, None, axis...  20.7 us
    all_gather x1, blocking collectives, local(): piece = lax.all_gather(act_grad, 'tile', axis=0, tiled=True)  16 us
    all_to_all x1, blocking collectives, local(): lax.all_to_all(feature_maps, 'tile', split_axis=0, concat_axis=2, tiled=T...  12.9 us
    dynamic_update_slice x5, local copies, waits for them, and re-layouts, forward_slot(): return lax.dynamic_update_slice_in_dim(buffer, result, slot * channels, 2)  12.2 us
    psum x1, waiting for transfers between devices, local(): lax.psum(weight_total.astype(jnp.bfloat16), ('col', 'rep'))  10.5 us
    ppermute x5, waiting for transfers between devices, extended_2(): lax.ppermute(lax.slice_in_dim(block, 0, width, axis=dim), axis, backward)  8.46 us
  transfers between devices with their start and end apart: 13, of which 9 were waited for; matrix products, arithmetic and copies ran while one was open for 14% of the time, Pallas kernels for 0%

profile of v1, /device:TPU:0, one launch (start us, length us, event | category | flops | bytes accessed | tf_op | source)
XLA Modules:
  0.0 235.2 jit_solution(18017784891626273623)
XLA Ops:
  8.2 4.9 %collective-permute-start = (bf16[1,5,32,64]{3,2,1,0:T(8,128)(2,1)S(1)}, bf16[1,5,32,64]{3,2,1,0:T(8,128)(2,1)S(1)}, u32[]{:S(2)}, u32[]{:S(2)}) collective-permute-start(bf16[1,5,32,64]{3,2,1,0:T(8,128)(2,1)S(1)} %get-tuple-element.229), channel_id=1, source_target_pairs={{0,2},{1,3},{4,6},{5,7},{8,10},{9,11},{12,14},{13,15},{16,18},{17,... | collective-permute-start | bytes 61448 | tf_op jit(solution)/shard_map/ppermute | solution.py:12
  13.0 1.3 collective-permute-start.1
  14.7 4.2 %collective-permute-done.1 = bf16[1,5,32,64]{3,2,1,0:T(8,128)(2,1)S(1)} collective-permute-done((bf16[1,5,32,64]{3,2,1,0:T(8,128)(2,1)S(1)}, bf16[1,5,32,64]{3,2,1,0:T(8,128)(2,1)S(1)}, u32[]{:S(2)}, u32[]{:S(2)}) %collective-permute-start.1) | collective-permute-done | bytes 20512 | tf_op jit(solution)/shard_map/ppermute | solution.py:15
  18.9 1.3 concatenate.55
  20.3 27.4 %while.24 = (s32[]{:T(128)}, bf16[32,16,320]{2,1,0:T(8,128)(2,1)S(1)}, s32[]{:T(128)}, bf16[5,32,1152]{2,1,0:T(8,128)(2,1)S(1)}, bf16[5,576,64]{1,2,0:T(8,128)(2...) while((s32[]{:T(128)}, bf16[32,16,320]{2,1,0:T(8,128)(2,1)S(1)}, s32[]{:T(128)}, ...), condition=%wide.region_1.2_spmd, body=%wide.region_0.1_spmd.sunk | while | flops 37912580 | bytes 3653833 | solution.py:74
  26.8 5.0 %dynamic_update_slice.16 = bf16[32,16,320]{2,1,0:T(8,128)(2,1)S(1)} dynamic-update-slice(bf16[32,16,320]{2,1,0:T(8,128)(2,1)S(1)} %get-tuple-element.369, bf16[32,16,64]{2,1,0:T(8,128)(2,1)S(1)} %bitcast.110, s32[]{:T(128)} %constant.90.clone.1..sunk, s32[]{:T(128)} %constant.90.clone.1..sunk, s32[]{:T(128)S(6)} %select_n.35) | dynamic-update-slice | bytes 131076 | tf_op jit(solution)/shard_map/while/body/dynamic_update_slice | solution.py:72
  38.5 5.0 %dynamic_update_slice.16 = bf16[32,16,320]{2,1,0:T(8,128)(2,1)S(1)} dynamic-update-slice(bf16[32,16,320]{2,1,0:T(8,128)(2,1)S(1)} %get-tuple-element.369, bf16[32,16,64]{2,1,0:T(8,128)(2,1)S(1)} %bitcast.110, s32[]{:T(128)} %constant.90.clone.1..sunk, s32[]{:T(128)} %constant.90.clone.1..sunk, s32[]{:T(128)S(6)} %select_n.35) | dynamic-update-slice | bytes 131076 | tf_op jit(solution)/shard_map/while/body/dynamic_update_slice | solution.py:72
  47.7 12.9 %all_to_all.15 = bf16[32,16,320]{2,1,0:T(8,128)(2,1)S(1)} all-to-all(bf16[32,16,320]{2,1,0:T(8,128)(2,1)S(1)} %get-tuple-element.153), channel_id=1, replica_groups=mesh['groups'=2,'tile'=4,'col'=2,'rep'=2] {'tile'}, dimensions={0} | all-to-all | bytes 655360 | tf_op jit(solution)/shard_map/all_to_all | solution.py:78
  61.3 1.7 convolution_convert_fusion.2
  63.0 1.4 collective-permute-start.3
  64.4 4.5 %collective-permute-start.2 = (bf16[1,16,512]{2,1,0:T(8,128)(2,1)S(1)}, bf16[1,16,512]{2,1,0:T(8,128)(2,1)S(1)}, u32[]{:S(2)}, u32[]{:S(2)}) collective-permute-start(bf16[1,16,512]{2,1,0:T(8,128)(2,1)S(1)} %get-tuple-element.240), channel_id=1, source_target_pairs={{0,4},{4,8},{8,12},{1,5},{5,9},{9,13},{2,6},{6,10},{10,14},{3,7},{... | collective-permute-start | bytes 49160 | tf_op jit(solution)/shard_map/ppermute | solution.py:12
  69.0 1.4 collective-permute-done.2
  70.4 1.9 collective-permute-start.4
  72.4 1.3 collective-permute-start.5
  73.8 4.2 %collective-permute-done.5 = bf16[10,1,512]{2,1,0:T(2,128)(2,1)S(1)} collective-permute-done((bf16[10,1,512]{2,1,0:T(2,128)(2,1)S(1)}, bf16[10,1,512]{2,1,0:T(2,128)(2,1)S(1)}, u32[]{:S(2)}, u32[]{:S(2)}) %collective-permute-start.5) | collective-permute-done | bytes 10272 | tf_op jit(solution)/shard_map/ppermute | solution.py:15
  81.5 4.8 %collective-permute-start.6 = (bf16[1,16,512]{2,1,0:T(8,128)(2,1)S(1)}, bf16[1,16,512]{2,1,0:T(8,128)(2,1)S(1)}, u32[]{:S(2)}, u32[]{:S(2)}) collective-permute-start(bf16[1,16,512]{2,1,0:T(8,128)(2,1)S(1)} %get-tuple-element.238), channel_id=1, source_target_pairs={{0,4},{4,8},{8,12},{1,5},{5,9},{9,13},{2,6},{6,10},{10,14},{3,7},{... | collective-permute-start | bytes 49160 | tf_op jit(solution)/shard_map/ppermute | solution.py:12
  86.4 1.4 collective-permute-done.6
  89.1 4.5 %collective-permute-start.9 = (bf16[10,1,512]{2,1,0:T(2,128)(2,1)S(1)}, bf16[10,1,512]{2,1,0:T(2,128)(2,1)S(1)}, u32[]{:S(2)}, u32[]{:S(2)}) collective-permute-start(bf16[10,1,512]{2,1,0:T(2,128)(2,1)S(1)} %get-tuple-element.233), channel_id=1, source_target_pairs={{0,2},{1,3},{4,6},{5,7},{8,10},{9,11},{12,14},{13,15},{16,18},{17,... | collective-permute-start | bytes 30728 | tf_op jit(solution)/shard_map/ppermute | solution.py:12
  93.7 1.5 collective-permute-done.9
  95.5 16.0 %all_gather.15 = bf16[32,16,512]{2,1,0:T(8,128)(2,1)S(1)} all-gather(bf16[8,16,512]{2,1,0:T(8,128)(2,1)S(1)} %fusion.44), channel_id=1, replica_groups=mesh['groups'=2,'tile'=4,'col'=2,'rep'=2] {'tile'}, dimensions={0}, use_global_device_ids=true | all-gather | bytes 655360 | tf_op jit(solution)/shard_map/all_gather | solution.py:131
  113.2 16.9 %while.25 = (s32[]{:T(128)}, bf16[5,576,64]{1,2,0:T(8,128)(2,1)S(1)}, s32[]{:T(128)}, bf16[5,32,1152]{2,1,0:T(8,128)(2,1)S(1)}, bf16[32,16,320]{2,1,0:T(8,128)(2...) while((s32[]{:T(128)}, ...), condition=%wide.region_15.16_spmd, body=%wide.region_14.15_spmd.sunk | while | flops 75825160 | bytes 4932813 | solution.py:154
  115.1 1.4 fusion.74
  118.3 1.4 fusion.74
  121.6 1.4 fusion.74
  124.8 1.4 fusion.74
  128.1 1.4 fusion.74
  132.3 1.3 copy.27
  133.7 20.8 %all-gather.1 = f32[16,9,512]{2,1,0:T(8,128)S(1)} all-gather(f32[1,9,512]{2,1,0:T(8,128)S(1)} %bitcast.123), channel_id=2, replica_groups=mesh['groups'=2,'tile'=4,'col'=2,'rep'=2] {'tile','col','rep'}, dimensions={0}, use_global_device_ids=true | all-gather | bytes 313344 | tf_op jit(solution)/shard_map/all_gather | solution.py:122
  156.2 10.5 %all-reduce.5.cloned.1.call-done = (bf16[320,512]{1,0:T(8,128)(2,1)}, bf16[5,576,64]{1,2,0:T(8,128)(2,1)}) async-done(((bf16[320,512]{1,0:T(8,128)(2,1)}, bf16[5,576,64]{1,2,0:T(8,128)(2,1)}), (bf16[320,512]{1,0:T(8,128)(2,1)}, bf16[5,576,64]{1,2,0:T(8,128)(2,1)})) %all-reduce.5.cloned.1.call-update) | async-done | bytes 696336 | tf_op jit(solution)/shard_map/psum | solution.py:141
  166.7 1.9 convert_element_type.146
  168.5 1.9 convert_element_type.149
  170.5 58.2 %reduce-scatter.4.cloned.1.call-done = f32[32,512]{1,0:T(8,128)} async-done(((f32[512,512]{1,0:T(8,128)}), f32[32,512]{1,0:T(8,128)}) %reduce-scatter.4.cloned.1.call-update) | async-done | bytes 65552
  (122 shorter events, 31.5 us)
Async XLA Ops:
  7.2 71.9 %copy-start = (bf16[512,512]{1,0:T(8,128)(2,1)S(1)}, bf16[512,512]{1,0:T(8,128)(2,1)}, u32[]{:S(2)}) copy-start(bf16[512,512]{1,0:T(8,128)(2,1)} %param.16) | copy-start | bytes 1572868
  7.2 54.1 %all-gather.4.cloned.1.call-start = ((), (), s32[]{:S(2)}) async-start(), calls=%async_computation.2 | async-start | bytes 1638400 | tf_op jit(solution)/shard_map/all_gather | solution.py:44
  8.2 6.5 %collective-permute-start = (bf16[1,5,32,64]{3,2,1,0:T(8,128)(2,1)S(1)}, bf16[1,5,32,64]{3,2,1,0:T(8,128)(2,1)S(1)}, u32[]{:S(2)}, u32[]{:S(2)}) collective-permute-start(bf16[1,5,32,64]{3,2,1,0:T(8,128)(2,1)S(1)} %get-tuple-element.229), channel_id=1, source_target_pairs={{0,2},{1,3},{4,6},{5,7},{8,10},{9,11},{12,14},{13,15},{16,18},{17,... | collective-permute-start | bytes 61448 | tf_op jit(solution)/shard_map/ppermute | solution.py:12
  13.0 5.9 %collective-permute-start.1 = (bf16[1,5,32,64]{3,2,1,0:T(8,128)(2,1)S(1)}, bf16[1,5,32,64]{3,2,1,0:T(8,128)(2,1)S(1)}, u32[]{:S(2)}, u32[]{:S(2)}) collective-permute-start(bf16[1,5,32,64]{3,2,1,0:T(8,128)(2,1)S(1)} %get-tuple-element.228), channel_id=1, source_target_pairs={{2,0},{3,1},{6,4},{7,5},{10,8},{11,9},{14,12},{15,13},{18,16},{19,... | collective-permute-start | bytes 61448 | tf_op jit(solution)/shard_map/ppermute | solution.py:15
  14.4 152.3 %all-reduce.5.cloned.1.call-start = ((), (), s32[]{:S(2)}) async-start(), calls=%async_computation.4 | async-start | bytes 1474560 | tf_op jit(solution)/shard_map/psum | solution.py:141
  60.9 12.7 %copy-start.5 = (f32[9,512]{1,0:T(8,128)S(1)}, f32[9,512]{1,0:T(8,128)}, u32[]{:S(2)}) copy-start(f32[9,512]{1,0:T(8,128)} %param.15) | copy-start | bytes 55300
  63.0 16.1 %copy-start.4 = (bf16[1,8,16,512]{3,2,1,0:T(8,128)(2,1)S(1)}, bf16[1,8,16,512]{3,2,1,0:T(8,128)(2,1)}, u32[]{:S(2)}) copy-start(bf16[1,8,16,512]{3,2,1,0:T(8,128)(2,1)} %param.17) | copy-start | bytes 393220
  63.0 6.0 %collective-permute-start.3 = (bf16[1,16,512]{2,1,0:T(8,128)(2,1)S(1)}, bf16[1,16,512]{2,1,0:T(8,128)(2,1)S(1)}, u32[]{:S(2)}, u32[]{:S(2)}) collective-permute-start(bf16[1,16,512]{2,1,0:T(8,128)(2,1)S(1)} %get-tuple-element.241), channel_id=1, source_target_pairs={{4,0},{8,4},{12,8},{5,1},{9,5},{13,9},{6,2},{10,6},{14,10},{7,3},{... | collective-permute-start | bytes 49160 | tf_op jit(solution)/shard_map/ppermute | solution.py:15
  64.4 6.0 %collective-permute-start.2 = (bf16[1,16,512]{2,1,0:T(8,128)(2,1)S(1)}, bf16[1,16,512]{2,1,0:T(8,128)(2,1)S(1)}, u32[]{:S(2)}, u32[]{:S(2)}) collective-permute-start(bf16[1,16,512]{2,1,0:T(8,128)(2,1)S(1)} %get-tuple-element.240), channel_id=1, source_target_pairs={{0,4},{4,8},{8,12},{1,5},{5,9},{9,13},{2,6},{6,10},{10,14},{3,7},{... | collective-permute-start | bytes 49160 | tf_op jit(solution)/shard_map/ppermute | solution.py:12
  70.4 3.4 %collective-permute-start.4 = (bf16[10,1,512]{2,1,0:T(2,128)(2,1)S(1)}, bf16[10,1,512]{2,1,0:T(2,128)(2,1)S(1)}, u32[]{:S(2)}, u32[]{:S(2)}) collective-permute-start(bf16[10,1,512]{2,1,0:T(2,128)(2,1)S(1)} %get-tuple-element.236), channel_id=1, source_target_pairs={{0,2},{1,3},{4,6},{5,7},{8,10},{9,11},{12,14},{13,15},{16,18},{17,... | collective-permute-start | bytes 30728 | tf_op jit(solution)/shard_map/ppermute | solution.py:12
  72.4 5.7 %collective-permute-start.5 = (bf16[10,1,512]{2,1,0:T(2,128)(2,1)S(1)}, bf16[10,1,512]{2,1,0:T(2,128)(2,1)S(1)}, u32[]{:S(2)}, u32[]{:S(2)}) collective-permute-start(bf16[10,1,512]{2,1,0:T(2,128)(2,1)S(1)} %get-tuple-element.237), channel_id=1, source_target_pairs={{2,0},{3,1},{6,4},{7,5},{10,8},{11,9},{14,12},{15,13},{18,16},{19,... | collective-permute-start | bytes 30728 | tf_op jit(solution)/shard_map/ppermute | solution.py:15
  80.2 6.1 %collective-permute-start.7 = (bf16[1,16,512]{2,1,0:T(8,128)(2,1)S(1)}, bf16[1,16,512]{2,1,0:T(8,128)(2,1)S(1)}, u32[]{:S(2)}, u32[]{:S(2)}) collective-permute-start(bf16[1,16,512]{2,1,0:T(8,128)(2,1)S(1)} %get-tuple-element.239), channel_id=1, source_target_pairs={{4,0},{8,4},{12,8},{5,1},{9,5},{13,9},{6,2},{10,6},{14,10},{7,3},{... | collective-permute-start | bytes 49160 | tf_op jit(solution)/shard_map/ppermute | solution.py:15
  81.5 6.3 %collective-permute-start.6 = (bf16[1,16,512]{2,1,0:T(8,128)(2,1)S(1)}, bf16[1,16,512]{2,1,0:T(8,128)(2,1)S(1)}, u32[]{:S(2)}, u32[]{:S(2)}) collective-permute-start(bf16[1,16,512]{2,1,0:T(8,128)(2,1)S(1)} %get-tuple-element.238), channel_id=1, source_target_pairs={{0,4},{4,8},{8,12},{1,5},{5,9},{9,13},{2,6},{6,10},{10,14},{3,7},{... | collective-permute-start | bytes 49160 | tf_op jit(solution)/shard_map/ppermute | solution.py:12
  87.8 5.9 %collective-permute-start.8 = (bf16[10,1,512]{2,1,0:T(2,128)(2,1)S(1)}, bf16[10,1,512]{2,1,0:T(2,128)(2,1)S(1)}, u32[]{:S(2)}, u32[]{:S(2)}) collective-permute-start(bf16[10,1,512]{2,1,0:T(2,128)(2,1)S(1)} %get-tuple-element.232), channel_id=1, source_target_pairs={{2,0},{3,1},{6,4},{7,5},{10,8},{11,9},{14,12},{15,13},{18,16},{19,... | collective-permute-start | bytes 30728 | tf_op jit(solution)/shard_map/ppermute | solution.py:15
  89.1 6.0 %collective-permute-start.9 = (bf16[10,1,512]{2,1,0:T(2,128)(2,1)S(1)}, bf16[10,1,512]{2,1,0:T(2,128)(2,1)S(1)}, u32[]{:S(2)}, u32[]{:S(2)}) collective-permute-start(bf16[10,1,512]{2,1,0:T(2,128)(2,1)S(1)} %get-tuple-element.233), channel_id=1, source_target_pairs={{0,2},{1,3},{4,6},{5,7},{8,10},{9,11},{12,14},{13,15},{16,18},{17,... | collective-permute-start | bytes 30728 | tf_op jit(solution)/shard_map/ppermute | solution.py:12
  111.5 1.1 copy-start.2
  130.2 0.8 copy-start.1
  131.0 97.7 %reduce-scatter.4.cloned.1.call-start = ((), (), s32[]{:S(2)}) async-start(), calls=%async_computation.3 | async-start | bytes 1114112
  132.3 1.4 copy-start.6
  132.3 1.4 copy-start.7
  132.3 1.4 copy-start.8
  133.6 21.6 %copy-start.3 = (bf16[8,16,512]{2,1,0:T(8,128)(2,1)S(1)}, bf16[8,16,512]{2,1,0:T(8,128)(2,1)}, u32[]{:S(2)}) copy-start(bf16[8,16,512]{2,1,0:T(8,128)(2,1)} %get-tuple-element.208) | copy-start | bytes 393220
Sparse Core Ops, SparseCore 0:
  14.5 34.9 all-gather.3
  131.1 35.5 all-reduce.4
  170.9 57.8 reduce-scatter.3
